TPU v7x, 32 devices: a whole 2x2x4 slice. The times are simulated.
32 devices in a mesh: dp: 16 (over z, x, core), ctx: 2 (over y).
Axes of the slice: x: 2, y: 2, z: 4, core: 2. Of those that a mesh axis runs over, the one named last changes fastest.
Arguments:
- queries: bfloat16 [16, 512, 2048], P('dp', 'ctx'), may hold values from -48 to 48
- key_store: bfloat16 [16, 512, 2048], P('dp', 'ctx'), may hold values from -4 to 4
- value_store: bfloat16 [16, 512, 2048], P('dp', 'ctx'), may hold values from -5 to 5
- kv_exponents: int32 [16, 4, 16], P('dp', 'ctx'), may hold values from -1 to 1
- valid_length: int32 [16], P('dp'), may hold values from 64 to 512, as said below
- round_index: int32 [1], replicated, may hold values from 0 to 63
- out_grad: bfloat16 [16, 512, 2048], P('dp', None, 'ctx'), may hold values from -6 to 6
- params: bfloat16 [16, 2048, 2048], P('dp', None, 'ctx'), may hold values from -6 to 6
- tracker: bfloat16 [16, 2048, 2048], P('dp', None, 'ctx'), may hold values from -6 to 6
- old_grad: bfloat16 [16, 2048, 2048], P('dp', None, 'ctx'), may hold values from -6 to 6
Outputs:
- new_params: bfloat16 [16, 2048, 2048], P('dp', None, 'ctx')
- new_tracker: bfloat16 [16, 2048, 2048], P('dp', None, 'ctx')
Inputs may be any that keep to these rules, and one draw needn't show every extreme that they name: `valid_length`: every draw has a replica whose clip fills all 512 positions.
All inputs are finite; a program needn't handle non-finite values.
Results may differ from a plain program's by a relative error of at most 0.0053.
Values may be sent and summed in bfloat16 or wider, within the bound.
A program may use at most 128 MiB of HBM per device.

v0:
```python
import functools

import jax
import jax.numpy as jnp
from jax import lax
from jax.experimental import pallas as pl
from jax.experimental.pallas import tpu as pltpu
from jax.sharding import PartitionSpec as P


HEADS = 16
HD = 128
KBLK = 128
QROWS = 256
LAST_ROWS = 256


step_size = 0.1
masked_score = -1e30


def from_partner(value, axis, bit):
    mask = 2**bit
    pairs = [(source, source ^ mask) for source in range(lax.axis_size(axis))]
    return lax.ppermute(value, axis, pairs)


def contract_rows(left_rows, right_rows):
    return lax.dot_general(
        left_rows, right_rows, (((0,), (0,)), ((), ())), preferred_element_type=jnp.float32
    )


def from_other(block):
    return lax.ppermute(block, "ctx", [(0, 1), (1, 0)])


def in_order(own, other, axis):
    first = lax.axis_index("ctx") == 0
    return jnp.concatenate(
        (jnp.where(first, own, other), jnp.where(first, other, own)), axis=axis
    )


def gather_ctx(block, axis):
    if lax.axis_size("ctx") != 2:
        return lax.all_gather(block, "ctx", axis=axis, tiled=True)
    return in_order(block, from_other(block), axis)


def rows_to_heads(block, group, groups):
    if lax.axis_size("ctx") != 2:
        return lax.all_to_all(block, "ctx", split_axis=1, concat_axis=0, tiled=True)
    width = block.shape[1] // (2 * groups)
    mine = lax.axis_index("ctx")
    kept = lax.dynamic_slice_in_dim(block, (mine * groups + group) * width, width, 1)
    sent = lax.dynamic_slice_in_dim(block, ((1 - mine) * groups + group) * width, width, 1)
    return in_order(kept, from_other(sent), 0)


def attend_kernel(step_heads, meta, scales, q_ref, k_ref, v_ref, out_ref):
    length = meta[0]
    seq = k_ref.shape[0]
    for local in range(step_heads):
        head = meta[1] + pl.program_id(0) * step_heads + local
        cols = pl.ds(local * HD, HD)

        def scaled(ref):
            return jnp.concatenate(
                [
                    (
                        ref[pl.ds(block * KBLK, KBLK), cols].astype(jnp.float32)
                        * scales[block, head]
                    ).astype(jnp.bfloat16)
                    for block in range(seq // KBLK)
                ],
                axis=0,
            )

        keys, values = scaled(k_ref), scaled(v_ref)
        for row0 in range(0, seq, QROWS):
            reach = row0 + QROWS
            scores = lax.dot_general(
                q_ref[pl.ds(row0, QROWS), cols],
                keys[:reach],
                (((1,), (1,)), ((), ())),
                preferred_element_type=jnp.float32,
            ) * (HD ** (-0.5))
            query_pos = row0 + lax.broadcasted_iota(jnp.int32, scores.shape, 0)
            key_pos = lax.broadcasted_iota(jnp.int32, scores.shape, 1)
            allowed = (key_pos <= query_pos) & (key_pos < length)
            scores = jnp.where(allowed, scores, masked_score)
            top = jnp.max(scores, axis=-1, keepdims=True)
            weights = jnp.exp(scores - top)
            total = jnp.sum(weights, axis=-1, keepdims=True)
            weighted = jnp.dot(
                weights.astype(jnp.bfloat16), values[:reach], preferred_element_type=jnp.float32
            )
            out_ref[pl.ds(row0, QROWS), cols] = (weighted / total).astype(jnp.bfloat16)


def attend(queries, keys, values, scales, length, first_head):
    seq, width = queries.shape
    heads = width // HD
    step_heads = 2 if heads % 2 == 0 and seq <= 512 else 1
    meta = jnp.stack((length, first_head)).astype(jnp.int32)
    spec = pl.BlockSpec((seq, step_heads * HD), lambda h: (0, h))
    smem = pl.BlockSpec(memory_space=pltpu.SMEM)
    return pl.pallas_call(
        functools.partial(attend_kernel, step_heads),
        grid=(heads // step_heads,),
        in_specs=[smem, smem, spec, spec, spec],
        out_specs=spec,
        out_shape=jax.ShapeDtypeStruct((seq, width), jnp.bfloat16),
        cost_estimate=pl.CostEstimate(
            flops=4 * seq * seq * width,
            bytes_accessed=8 * seq * width,
            transcendentals=seq * seq * heads,
        ),
    )(meta, scales, queries, keys, values)


def average_kernel(own_ref, peer_ref, tracker_ref, *rest):
    out_ref = rest[-1]
    out_ref[...] = (
        0.5 * (own_ref[...].astype(jnp.float32) + peer_ref[...].astype(jnp.float32))
        - step_size * tracker_ref[...].astype(jnp.float32)
    ).astype(jnp.bfloat16)


def average_rows(own, peer_rows, new_tracker, start, filled=None):
    rows, cols = peer_rows.shape
    tile = LAST_ROWS
    here = pl.BlockSpec((tile, cols), lambda i: (i + start // tile, 0))
    operands = [own, peer_rows, new_tracker]
    specs = [here, pl.BlockSpec((tile, cols), lambda i: (i, 0)), here]
    aliases = {}
    if filled is not None:
        operands.append(filled)
        specs.append(pl.BlockSpec(memory_space=pl.ANY))
        aliases = {3: 0}
    return pl.pallas_call(
        average_kernel,
        grid=(rows // tile,),
        in_specs=specs,
        out_specs=here,
        out_shape=jax.ShapeDtypeStruct(own.shape, jnp.bfloat16),
        input_output_aliases=aliases,
        cost_estimate=pl.CostEstimate(
            flops=4 * rows * cols, bytes_accessed=8 * rows * cols, transcendentals=0
        ),
    )(*operands)


def step_with(bit_number):
    def step(
        queries, key_store, value_store, kv_exponents, valid_length,
        out_grad, params, tracker, old_grad,
    ):
        split = params.shape[1] - LAST_ROWS
        peer_tracker = from_partner(tracker[0], "dp", bit_number)
        peer_most = from_partner(params[0, :split], "dp", bit_number)
        peer_last = from_partner(params[0, split:], "dp", bit_number)
        length = valid_length[0]
        seq_rows = out_grad.shape[1]
        live_rows = jnp.arange(seq_rows)[:, None] < length
        masked = jnp.where(live_rows, out_grad[0], jnp.zeros((), jnp.bfloat16))
        groups = 2 if lax.axis_size("ctx") == 2 else 1
        exponents = gather_ctx(kv_exponents[0], 0)
        pieces = [
            [
                rows_to_heads(block[0], group, groups)
                for block in (key_store, value_store, queries)
            ]
            for group in range(groups)
        ]
        scales = jnp.exp2(exponents.astype(jnp.float32))
        group_heads = HEADS // (lax.axis_size("ctx") * groups)
        parts = []
        for group, (keys, values, rows) in enumerate(pieces):
            first_head = (lax.axis_index("ctx") * groups + group) * group_heads
            own = attend(rows, keys, values, scales, length, first_head)
            parts.append(gather_ctx(own, 1))
        if groups == 1:
            attended = parts[0]
        else:
            width = group_heads * HD
            attended = jnp.concatenate(
                [
                    part[:, side * width : (side + 1) * width]
                    for side in range(2)
                    for part in parts
                ],
                axis=1,
            )
        grad_new = contract_rows(attended, masked)
        tracker_sum = (
            0.5 * (tracker[0].astype(jnp.float32) + peer_tracker.astype(jnp.float32))
            + grad_new
            - old_grad[0].astype(jnp.float32)
        )
        new_tracker = tracker_sum.astype(jnp.bfloat16)
        new_params = average_rows(params[0], peer_most, new_tracker, 0)
        new_params = average_rows(params[0], peer_last, new_tracker, split, new_params)
        return (new_params[None], new_tracker[None])

    return step


def shards(
    queries,
    key_store,
    value_store,
    kv_exponents,
    valid_length,
    round_index,
    out_grad,
    params,
    tracker,
    old_grad,
):
    levels = lax.axis_size("dp").bit_length() - 1
    bit_now = round_index[0] % levels
    return lax.switch(
        bit_now,
        [step_with(bit_number) for bit_number in range(levels)],
        queries, key_store, value_store, kv_exponents, valid_length,
        out_grad, params, tracker, old_grad,
    )


def solution(mesh):
    placed = (
        P("dp", "ctx", None),
        P("dp", "ctx", None),
        P("dp", "ctx", None),
        P("dp", "ctx", None),
        P("dp"),
        P(),
        P("dp", None, "ctx"),
        P("dp", None, "ctx"),
        P("dp", None, "ctx"),
        P("dp", None, "ctx"),
    )
    return jax.shard_map(
        shards,
        mesh=mesh,
        in_specs=placed,
        out_specs=(P("dp", None, "ctx"), P("dp", None, "ctx")),
        check_vma=False,
    )
```

profile of v0, /device:TPU:0, one launch (start us, length us, event | category | flops | bytes accessed | tf_op | source)
XLA Modules:
  0.0 369.6 jit_solution(7248049229301375195)
XLA Ops:
  1.3 368.3 %conditional.1 = (bf16[1,2048,1024]{2,1,0:T(8,128)(2,1)}, bf16[1,2048,1024]{2,1,0:T(8,128)(2,1)}) conditional(s32[]{:T(128)} %clamp.3, (bf16[1,2048,1024]{2,1,0:T(8,128)(2,1)}, bf16[1,2048,1024]{2,1,0:T(8,128)(2,1)}, s32[1]{0:T(128)}, s32[1,2,16]{2,1,0:T(2,128)}, bf16[1,256,2048]{2,1,0:T(8,128)(2,1)}, ...), branch_computations={%region_0.1_spmd, %region_1.2_spmd, %region_2.3_spmd, %region_3.4_... | conditional | flops 3264217856 | bytes 154144912 | solution.py:224
  1.8 4.1 %collective-permute-start.37 = (bf16[2048,1024]{1,0:T(8,128)(2,1)}, bf16[2048,1024]{1,0:T(8,128)(2,1)}, u32[]{:S(2)}, u32[]{:S(2)}) collective-permute-start(bf16[2048,1024]{1,0:T(8,128)(2,1)} %bitcast.231), channel_id=1, source_target_pairs={{0,16},{2,18},{4,20},{6,22},{8,24},{10,26},{12,28},{14,30},{16,0},... | collective-permute-start | bytes 12582920 | tf_op jit(solution)/shard_map/cond/branch_3_fun/ppermute | solution.py:25
  5.9 1.5 collective-permute-start.38
  7.5 1.9 dynamic-slice_bitcast_fusion.23
  9.3 0.5 collective-permute-start.39
  9.8 1.5 collective-permute-start.43
  11.4 1.9 dynamic-slice_bitcast_fusion.22
  13.2 0.5 collective-permute-start.40
  13.7 1.3 pad_add_fusion.7.meta
  15.0 1.3 pad_add_fusion.6.meta
  16.3 2.0 dynamic-slice_bitcast_fusion.21
  18.3 4.4 %slice_bitcast_fusion.6 = bf16[1792,1024]{1,0:T(8,128)(2,1)} fusion(bf16[1,2048,1024]{2,1,0:T(8,128)(2,1)} %get-tuple-element.99), kind=kLoop, calls=%fused_computation.161 | loop fusion | bytes 7340032 | tf_op jit(solution)/shard_map/cond/branch_3_fun/squeeze | solution.py:162
  22.7 0.1 collective-permute-start.47
  22.8 0.6 fusion.65.scales
  23.3 1.8 collective-permute-start.44
  25.1 0.3 collective-permute-start.41
  25.4 4.6 %collective-permute-done.40 = bf16[256,512]{1,0:T(8,128)(2,1)S(1)} collective-permute-done((bf16[256,512]{1,0:T(8,128)(2,1)}, bf16[256,512]{1,0:T(8,128)(2,1)S(1)}, u32[]{:S(2)}, u32[]{:S(2)}) %collective-permute-start.40) | collective-permute-done | bytes 262176 | tf_op jit(solution)/shard_map/cond/branch_3_fun/ppermute | solution.py:35
  30.0 0.7 copy-done.31
  30.7 0.5 collective-permute-start.45
  31.2 1.9 bitcast_select_fusion.55
  33.1 0.8 pad_maximum_fusion.18.q_ref
  34.0 1.6 collective-permute-done.44
  35.6 5.6 %collective-permute-done.41 = bf16[256,512]{1,0:T(8,128)(2,1)S(1)} collective-permute-done((bf16[256,512]{1,0:T(8,128)(2,1)}, bf16[256,512]{1,0:T(8,128)(2,1)S(1)}, u32[]{:S(2)}, u32[]{:S(2)}) %collective-permute-start.41) | collective-permute-done | bytes 262176 | tf_op jit(solution)/shard_map/cond/branch_3_fun/ppermute | solution.py:35
  41.2 3.9 %collective-permute-done.45 = bf16[256,512]{1,0:T(8,128)(2,1)S(1)} collective-permute-done((bf16[256,512]{1,0:T(8,128)(2,1)}, bf16[256,512]{1,0:T(8,128)(2,1)S(1)}, u32[]{:S(2)}, u32[]{:S(2)}) %collective-permute-start.45) | collective-permute-done | bytes 262176 | tf_op jit(solution)/shard_map/cond/branch_3_fun/ppermute | solution.py:35
  45.1 2.1 bitcast_select_fusion.51
  47.3 0.8 pad_maximum_fusion.20.v_ref
  48.1 0.8 pad_maximum_fusion.19.k_ref
  48.9 4.6 %branch_3_fun.4 = bf16[512,512]{1,0:T(8,128)(2,1)} custom-call(s32[2]{0:T(128)} %pad_add_fusion.6.meta, f32[4,16]{1,0:T(4,128)} %fusion.65.scales, bf16[512,512]{1,0:T(8,128)(2,1)} %pad_maximum_fusion.18.q_ref, bf16[512,512]{1,0:T(8,128)(2,1)} %pad_maximum_fusion.19.k_ref, bf16[512,512]{1,0:T(8,128)(2,1)} %pad_maximum_fusion.20.v_ref), custom_call_target="tpu_custom_call" | custom-call | flops 536870912 | bytes 2097152 | tf_op jit(solution)/shard_map/cond/branch_3_fun/pallas_call | solution.py:109
  53.5 0.5 collective-permute-start.42
  54.1 0.8 pad_maximum_fusion.21.q_ref
  54.9 0.8 pad_maximum_fusion.23.v_ref
  55.7 0.8 pad_maximum_fusion.22.k_ref
  56.6 4.7 %branch_3_fun.5 = bf16[512,512]{1,0:T(8,128)(2,1)} custom-call(s32[2]{0:T(128)} %pad_add_fusion.7.meta, f32[4,16]{1,0:T(4,128)} %fusion.65.scales, bf16[512,512]{1,0:T(8,128)(2,1)} %pad_maximum_fusion.21.q_ref, bf16[512,512]{1,0:T(8,128)(2,1)} %pad_maximum_fusion.22.k_ref, bf16[512,512]{1,0:T(8,128)(2,1)} %pad_maximum_fusion.23.v_ref), custom_call_target="tpu_custom_call" | custom-call | flops 536870912 | bytes 2097152 | tf_op jit(solution)/shard_map/cond/branch_3_fun/pallas_call | solution.py:109
  61.3 1.5 collective-permute-start.46
  62.8 1.1 slice_bitcast_fusion.7
  63.9 0.4 collective-permute-start.36
  64.3 0.6 iota_compare_fusion.3
  64.9 3.6 collective-permute-done.42
  68.6 0.1 broadcast_select_fusion.21
  68.6 8.7 %collective-permute-done.46 = bf16[512,512]{1,0:T(8,128)(2,1)S(1)} collective-permute-done((bf16[512,512]{1,0:T(8,128)(2,1)}, bf16[512,512]{1,0:T(8,128)(2,1)S(1)}, u32[]{:S(2)}, u32[]{:S(2)}) %collective-permute-start.46) | collective-permute-done | bytes 524320 | tf_op jit(solution)/shard_map/cond/branch_3_fun/ppermute | solution.py:35
  77.3 1.1 broadcast_select_fusion.20
  78.5 199.0 %collective-permute-done.37 = bf16[2048,1024]{1,0:T(8,128)(2,1)} collective-permute-done((bf16[2048,1024]{1,0:T(8,128)(2,1)}, bf16[2048,1024]{1,0:T(8,128)(2,1)}, u32[]{:S(2)}, u32[]{:S(2)}) %collective-permute-start.37) | collective-permute-done | bytes 4194336 | tf_op jit(solution)/shard_map/cond/branch_3_fun/ppermute | solution.py:25
  277.4 8.2 %fusion.51.tracker_ref = bf16[2048,1024]{1,0:T(8,128)(2,1)} fusion(bf16[2048,1024]{1,0:T(8,128)(2,1)} %collective-permute-done.37, bf16[1,2048,1024]{2,1,0:T(8,128)(2,1)} %get-tuple-element.107, bf16[512,512]{1,0:T(8,128)(2,1)S(1)} %get-tuple-element.229, bf16[512,512]{1,0:T(8,128)(2,1)S(1)} %get-tuple-element.227, ...), kind=kOutput, calls=%fused_computation.160 | convolution fusion | flops 2173173760 | bytes 19923456 | tf_op jit(solution)/shard_map/cond/branch_3_fun/dot_general | solution.py:29
  285.6 70.5 %collective-permute-done.47.peer_ref = bf16[1792,1024]{1,0:T(8,128)(2,1)} collective-permute-done((bf16[1792,1024]{1,0:T(8,128)(2,1)}, bf16[1792,1024]{1,0:T(8,128)(2,1)}, u32[]{:S(2)}, u32[]{:S(2)}) %collective-permute-start.47) | collective-permute-done | bytes 3670048 | tf_op jit(solution)/shard_map/cond/branch_3_fun/ppermute | solution.py:25
  356.1 8.6 %branch_3_fun.6.rest_0_ = bf16[2048,1024]{1,0:T(8,128)(2,1)} custom-call(bf16[2048,1024]{1,0:T(8,128)(2,1)} %bitcast.214, bf16[1792,1024]{1,0:T(8,128)(2,1)} %collective-permute-done.47.peer_ref, bf16[2048,1024]{1,0:T(8,128)(2,1)} %fusion.51.tracker_ref), custom_call_target="tpu_custom_call" | custom-call | flops 7340032 | bytes 14680064 | tf_op jit(solution)/shard_map/cond/branch_3_fun/pallas_call | solution.py:142
  364.7 1.7 collective-permute-done.36.peer_ref
  366.4 0.8 copy-done.27
  367.2 2.4 branch_3_fun.7
  (24 shorter events, 0.0 us)
Async XLA Ops:
  1.8 275.6 %collective-permute-start.37 = (bf16[2048,1024]{1,0:T(8,128)(2,1)}, bf16[2048,1024]{1,0:T(8,128)(2,1)}, u32[]{:S(2)}, u32[]{:S(2)}) collective-permute-start(bf16[2048,1024]{1,0:T(8,128)(2,1)} %bitcast.231), channel_id=1, source_target_pairs={{0,16},{2,18},{4,20},{6,22},{8,24},{10,26},{12,28},{14,30},{16,0},... | collective-permute-start | bytes 12582920 | tf_op jit(solution)/shard_map/cond/branch_3_fun/ppermute | solution.py:25
  5.9 16.7 %collective-permute-start.38 = (s32[2,16]{1,0:T(2,128)}, s32[2,16]{1,0:T(2,128)S(1)}, u32[]{:S(2)}, u32[]{:S(2)}) collective-permute-start(s32[2,16]{1,0:T(2,128)} %bitcast.227), channel_id=1, source_target_pairs={{0,1},{1,0},{2,3},{3,2},{4,5},{5,4},{6,7},{7,6},{8,9},{9,8},{10,11... | collective-permute-start | bytes 392 | tf_op jit(solution)/shard_map/cond/branch_3_fun/ppermute | solution.py:35
  9.3 14.0 %collective-permute-start.39 = (bf16[256,512]{1,0:T(8,128)(2,1)}, bf16[256,512]{1,0:T(8,128)(2,1)}, u32[]{:S(2)}, u32[]{:S(2)}) collective-permute-start(bf16[256,512]{1,0:T(8,128)(2,1)} %get-tuple-element.240), channel_id=1, source_target_pairs={{0,1},{1,0},{2,3},{3,2},{4,5},{5,4},{6,7},{7,6},{8,9},{9,8},{10,11... | collective-permute-start | bytes 786440 | tf_op jit(solution)/shard_map/cond/branch_3_fun/ppermute | solution.py:35
  9.8 15.3 %collective-permute-start.43 = (bf16[256,512]{1,0:T(8,128)(2,1)}, bf16[256,512]{1,0:T(8,128)(2,1)}, u32[]{:S(2)}, u32[]{:S(2)}) collective-permute-start(bf16[256,512]{1,0:T(8,128)(2,1)} %get-tuple-element.241), channel_id=1, source_target_pairs={{0,1},{1,0},{2,3},{3,2},{4,5},{5,4},{6,7},{7,6},{8,9},{9,8},{10,11... | collective-permute-start | bytes 786440 | tf_op jit(solution)/shard_map/cond/branch_3_fun/ppermute | solution.py:35
  13.2 16.7 %collective-permute-start.40 = (bf16[256,512]{1,0:T(8,128)(2,1)}, bf16[256,512]{1,0:T(8,128)(2,1)S(1)}, u32[]{:S(2)}, u32[]{:S(2)}) collective-permute-start(bf16[256,512]{1,0:T(8,128)(2,1)} %get-tuple-element.236), channel_id=1, source_target_pairs={{0,1},{1,0},{2,3},{3,2},{4,5},{5,4},{6,7},{7,6},{8,9},{9,8},{10,11... | collective-permute-start | bytes 786440 | tf_op jit(solution)/shard_map/cond/branch_3_fun/ppermute | solution.py:35
  16.3 6.5 %copy-start.35 = (s32[1,2,16]{2,1,0:T(2,128)S(1)}, s32[1,2,16]{2,1,0:T(2,128)}, u32[]{:S(2)}) copy-start(s32[1,2,16]{2,1,0:T(2,128)} %get-tuple-element.102) | copy-start | bytes 388 | tf_op jit(solution)/shard_map/cond
  16.3 14.9 %copy-start.11 = (bf16[1,256,2048]{2,1,0:T(8,128)(2,1)S(1)}, bf16[1,256,2048]{2,1,0:T(8,128)(2,1)}, u32[]{:S(2)}) copy-start(bf16[1,256,2048]{2,1,0:T(8,128)(2,1)} %get-tuple-element.103) | copy-start | bytes 3145732 | tf_op jit(solution)/shard_map/cond
  18.3 26.8 %copy-start.3 = (bf16[1,256,2048]{2,1,0:T(8,128)(2,1)S(1)}, bf16[1,256,2048]{2,1,0:T(8,128)(2,1)}, u32[]{:S(2)}) copy-start(bf16[1,256,2048]{2,1,0:T(8,128)(2,1)} %get-tuple-element.104) | copy-start | bytes 3145732 | tf_op jit(solution)/shard_map/cond
  18.3 26.8 %copy-start.7 = (bf16[1,256,2048]{2,1,0:T(8,128)(2,1)S(1)}, bf16[1,256,2048]{2,1,0:T(8,128)(2,1)}, u32[]{:S(2)}) copy-start(bf16[1,256,2048]{2,1,0:T(8,128)(2,1)} %get-tuple-element.105) | copy-start | bytes 3145732 | tf_op jit(solution)/shard_map/cond
  22.7 333.4 %collective-permute-start.47 = (bf16[1792,1024]{1,0:T(8,128)(2,1)}, bf16[1792,1024]{1,0:T(8,128)(2,1)}, u32[]{:S(2)}, u32[]{:S(2)}) collective-permute-start(bf16[1792,1024]{1,0:T(8,128)(2,1)} %slice_bitcast_fusion.6), channel_id=1, source_target_pairs={{0,16},{2,18},{4,20},{6,22},{8,24},{10,26},{12,28},{14,30},{16,0},... | collective-permute-start | bytes 11010056 | tf_op jit(solution)/shard_map/cond/branch_3_fun/ppermute | solution.py:25
  23.3 12.2 %collective-permute-start.44 = (bf16[256,512]{1,0:T(8,128)(2,1)}, bf16[256,512]{1,0:T(8,128)(2,1)S(1)}, u32[]{:S(2)}, u32[]{:S(2)}) collective-permute-start(bf16[256,512]{1,0:T(8,128)(2,1)} %get-tuple-element.237), channel_id=1, source_target_pairs={{0,1},{1,0},{2,3},{3,2},{4,5},{5,4},{6,7},{7,6},{8,9},{9,8},{10,11... | collective-permute-start | bytes 786440 | tf_op jit(solution)/shard_map/cond/branch_3_fun/ppermute | solution.py:35
  25.1 16.1 %collective-permute-start.41 = (bf16[256,512]{1,0:T(8,128)(2,1)}, bf16[256,512]{1,0:T(8,128)(2,1)S(1)}, u32[]{:S(2)}, u32[]{:S(2)}) collective-permute-start(bf16[256,512]{1,0:T(8,128)(2,1)} %get-tuple-element.232), channel_id=1, source_target_pairs={{0,1},{1,0},{2,3},{3,2},{4,5},{5,4},{6,7},{7,6},{8,9},{9,8},{10,11... | collective-permute-start | bytes 786440 | tf_op jit(solution)/shard_map/cond/branch_3_fun/ppermute | solution.py:35
  30.0 0.7 copy-start.31
  30.7 14.4 %collective-permute-start.45 = (bf16[256,512]{1,0:T(8,128)(2,1)}, bf16[256,512]{1,0:T(8,128)(2,1)S(1)}, u32[]{:S(2)}, u32[]{:S(2)}) collective-permute-start(bf16[256,512]{1,0:T(8,128)(2,1)} %get-tuple-element.233), channel_id=1, source_target_pairs={{0,1},{1,0},{2,3},{3,2},{4,5},{5,4},{6,7},{7,6},{8,9},{9,8},{10,11... | collective-permute-start | bytes 786440 | tf_op jit(solution)/shard_map/cond/branch_3_fun/ppermute | solution.py:35
  34.0 20.1 %copy-start.19 = (bf16[256,512]{1,0:T(8,128)(2,1)S(1)}, bf16[256,512]{1,0:T(8,128)(2,1)}, u32[]{:S(2)}) copy-start(bf16[256,512]{1,0:T(8,128)(2,1)} %get-tuple-element.239) | copy-start | bytes 786436 | tf_op jit(solution)/shard_map/cond
  47.3 7.6 %copy-start.23 = (bf16[256,512]{1,0:T(8,128)(2,1)S(1)}, bf16[256,512]{1,0:T(8,128)(2,1)}, u32[]{:S(2)}) copy-start(bf16[256,512]{1,0:T(8,128)(2,1)} %get-tuple-element.231) | copy-start | bytes 786436 | tf_op jit(solution)/shard_map/cond
  53.5 15.0 %copy-start.15 = (bf16[512,512]{1,0:T(8,128)(2,1)S(1)}, bf16[512,512]{1,0:T(8,128)(2,1)}, u32[]{:S(2)}) copy-start(bf16[512,512]{1,0:T(8,128)(2,1)} %branch_3_fun.4) | copy-start | bytes 1572868 | tf_op jit(solution)/shard_map/cond
  53.5 15.0 %collective-permute-start.42 = (bf16[512,512]{1,0:T(8,128)(2,1)}, bf16[512,512]{1,0:T(8,128)(2,1)S(1)}, u32[]{:S(2)}, u32[]{:S(2)}) collective-permute-start(bf16[512,512]{1,0:T(8,128)(2,1)} %branch_3_fun.4), channel_id=1, source_target_pairs={{0,1},{1,0},{2,3},{3,2},{4,5},{5,4},{6,7},{7,6},{8,9},{9,8},{10,11... | collective-permute-start | bytes 1572872 | tf_op jit(solution)/shard_map/cond/branch_3_fun/ppermute | solution.py:35
  56.6 220.9 %copy-start.43 = (bf16[1,512,1024]{2,1,0:T(8,128)(2,1)S(1)}, bf16[1,512,1024]{2,1,0:T(8,128)(2,1)}, u32[]{:S(2)}) copy-start(bf16[1,512,1024]{2,1,0:T(8,128)(2,1)} %get-tuple-element.106) | copy-start | bytes 3145732 | tf_op jit(solution)/shard_map/cond
  61.3 216.2 %copy-start.39 = (bf16[1,2048,1024]{2,1,0:T(8,128)(2,1)S(1)}, bf16[1,2048,1024]{2,1,0:T(8,128)(2,1)}, u32[]{:S(2)}) copy-start(bf16[1,2048,1024]{2,1,0:T(8,128)(2,1)} %get-tuple-element.100) | copy-start | bytes 12582916 | tf_op jit(solution)/shard_map/cond
  61.3 16.1 %collective-permute-start.46 = (bf16[512,512]{1,0:T(8,128)(2,1)}, bf16[512,512]{1,0:T(8,128)(2,1)S(1)}, u32[]{:S(2)}, u32[]{:S(2)}) collective-permute-start(bf16[512,512]{1,0:T(8,128)(2,1)} %branch_3_fun.5), channel_id=1, source_target_pairs={{0,1},{1,0},{2,3},{3,2},{4,5},{5,4},{6,7},{7,6},{8,9},{9,8},{10,11... | collective-permute-start | bytes 1572872 | tf_op jit(solution)/shard_map/cond/branch_3_fun/ppermute | solution.py:35
  63.9 302.5 %collective-permute-start.36 = (bf16[256,1024]{1,0:T(8,128)(2,1)S(1)}, bf16[256,1024]{1,0:T(8,128)(2,1)S(1)}, u32[]{:S(2)}, u32[]{:S(2)}) collective-permute-start(bf16[256,1024]{1,0:T(8,128)(2,1)S(1)} %slice_bitcast_fusion.7), channel_id=1, source_target_pairs={{0,16},{2,18},{4,20},{6,22},{8,24},{10,26},{12,28},{14,30},{16,0},... | collective-permute-start | bytes 1572872 | tf_op jit(solution)/shard_map/cond/branch_3_fun/ppermute | solution.py:25
  366.4 0.8 copy-start.27
where the time goes:
time: 370 us
  waiting for transfers between devices  299 us (81%)
  Pallas kernels  20.3 us (5%)
  other arithmetic  14.1 us (4%)
  starting transfers between devices  13.2 us (4%)
  local copies, waits for them, and re-layouts  12.7 us (3%)
  matrix products  8.15 us (2%)
    ppermute x3, waiting for transfers between devices, from_partner(): return lax.ppermute(value, axis, pairs)  271 us
    ppermute x9, waiting for transfers between devices, from_other(): return lax.ppermute(block, 'ctx', [(0, 1), (1, 0)])  28.1 us
    pallas_call x2, Pallas kernels, average_rows(): pl.pallas_call(average_kernel, grid=(rows // tile,), in_specs=specs, out_...  11 us
    pallas_call x2, Pallas kernels, attend(): pl.pallas_call(functools.partial(attend_kernel, step_heads), grid=(heads...  9.31 us
    ppermute x9, starting transfers between devices, from_other(): return lax.ppermute(block, 'ctx', [(0, 1), (1, 0)])  8.6 us
    dot_general x1, matrix products, contract_rows(): lax.dot_general(left_rows, right_rows, (((0,), (0,)), ((), ())), preferre...  8.15 us
  transfers between devices with their start and end apart: 12, of which 9 were waited for; matrix products, arithmetic and copies ran while one was open for 9% of the time, Pallas kernels for 5%

commit v1 on v0

--- a/solution.py
+++ b/solution.py
@@ -13,6 +13,7 @@
 KBLK = 128
 QROWS = 256
 LAST_ROWS = 256
+COMBINE_ROWS = 256
 
 
 step_size = 0.1
@@ -133,7 +134,10 @@
     tile = LAST_ROWS
     here = pl.BlockSpec((tile, cols), lambda i: (i + start // tile, 0))
     operands = [own, peer_rows, new_tracker]
-    specs = [here, pl.BlockSpec((tile, cols), lambda i: (i, 0)), here]
+    peer_spec = pl.BlockSpec((tile, cols), lambda i: (i, 0))
+    if rows == tile:
+        peer_spec = pl.BlockSpec(memory_space=pltpu.VMEM)
+    specs = [here, peer_spec, here]
     aliases = {}
     if filled is not None:
         operands.append(filled)
@@ -152,39 +156,104 @@
     )(*operands)
 
 
+def combine_kernel(base, att_ref, masked_ref, tracker_ref, peer_tracker_ref, old_ref,
+                   params_ref, peer_params_ref, *rest):
+    new_tracker_ref, new_params_ref = rest[-2:]
+    grad = contract_rows(att_ref[...], masked_ref[...])
+    new_tracker = (
+        0.5 * (tracker_ref[...].astype(jnp.float32) + peer_tracker_ref[...].astype(jnp.float32))
+        + grad
+        - old_ref[...].astype(jnp.float32)
+    ).astype(jnp.bfloat16)
+    new_tracker_ref[...] = new_tracker
+    new_params_ref[...] = (
+        0.5 * (params_ref[...].astype(jnp.float32) + peer_params_ref[...].astype(jnp.float32))
+        - step_size * new_tracker.astype(jnp.float32)
+    ).astype(jnp.bfloat16)
+
+
+def combine_rows(part, row_start, masked, arrays, filled):
+    seq, width = part.shape
+    cols = masked.shape[1]
+    tile = COMBINE_ROWS
+    here = pl.BlockSpec((tile, cols), lambda i, base: (base[0] + i, 0))
+    specs = [
+        pl.BlockSpec((seq, tile), lambda i, base: (0, i)),
+        pl.BlockSpec((seq, cols), lambda i, base: (0, 0)),
+    ] + [here] * len(arrays)
+    aliases = {}
+    if filled:
+        specs += [pl.BlockSpec(memory_space=pl.ANY)] * 2
+        aliases = {3 + len(arrays): 0, 4 + len(arrays): 1}
+    shape = jax.ShapeDtypeStruct(arrays[0].shape, jnp.bfloat16)
+    return pl.pallas_call(
+        combine_kernel,
+        grid_spec=pltpu.PrefetchScalarGridSpec(
+            num_scalar_prefetch=1,
+            grid=(width // tile,),
+            in_specs=specs,
+            out_specs=[here, here],
+        ),
+        out_shape=[shape, shape],
+        input_output_aliases=aliases,
+        cost_estimate=pl.CostEstimate(
+            flops=2 * seq * width * cols,
+            bytes_accessed=2 * (7 * width * cols + seq * cols + seq * width),
+            transcendentals=0,
+        ),
+    )((row_start // tile).astype(jnp.int32)[None], part, masked, *arrays, *filled)
+
+
 def step_with(bit_number):
     def step(
         queries, key_store, value_store, kv_exponents, valid_length,
         out_grad, params, tracker, old_grad,
     ):
+        by_group = bit_number == 0 and lax.axis_size("ctx") == 2
         split = params.shape[1] - LAST_ROWS
         peer_tracker = from_partner(tracker[0], "dp", bit_number)
-        peer_most = from_partner(params[0, :split], "dp", bit_number)
-        peer_last = from_partner(params[0, split:], "dp", bit_number)
+        if by_group:
+            peer_params = from_partner(params[0], "dp", bit_number)
+        else:
+            peer_most = from_partner(params[0, :split], "dp", bit_number)
+            peer_last = from_partner(params[0, split:], "dp", bit_number)
         length = valid_length[0]
         seq_rows = out_grad.shape[1]
         live_rows = jnp.arange(seq_rows)[:, None] < length
         masked = jnp.where(live_rows, out_grad[0], jnp.zeros((), jnp.bfloat16))
         groups = 2 if lax.axis_size("ctx") == 2 else 1
         exponents = gather_ctx(kv_exponents[0], 0)
-        pieces = [
-            [
-                rows_to_heads(block[0], group, groups)
-                for block in (key_store, value_store, queries)
-            ]
-            for group in range(groups)
+        scales = jnp.exp2(exponents.astype(jnp.float32))
+        pieces = []
+        for group in range(groups):
+            pieces.append(
+                [
+                    rows_to_heads(block[0], group, groups)
+                    for block in (key_store, value_store, queries)
+                ]
+            )
+        mine = lax.axis_index("ctx")
+        group_heads = HEADS // (lax.axis_size("ctx") * groups)
+        width = group_heads * HD
+        own_parts = [
+            attend(rows, keys, values, scales, length, (mine * groups + group) * group_heads)
+            for group, (keys, values, rows) in enumerate(pieces)
         ]
-        scales = jnp.exp2(exponents.astype(jnp.float32))
-        group_heads = HEADS // (lax.axis_size("ctx") * groups)
-        parts = []
-        for group, (keys, values, rows) in enumerate(pieces):
-            first_head = (lax.axis_index("ctx") * groups + group) * group_heads
-            own = attend(rows, keys, values, scales, length, first_head)
-            parts.append(gather_ctx(own, 1))
+        if by_group:
+            arrays = (tracker[0], peer_tracker, old_grad[0], params[0], peer_params)
+            done = ()
+            other_parts = []
+            for own in own_parts:
+                other_parts.append(from_other(own))
+            for side, parts in ((mine, own_parts), (1 - mine, other_parts)):
+                for group, part in enumerate(parts):
+                    row_start = (side * groups + group) * width
+                    done = combine_rows(part, row_start, masked, arrays, done)
+            return (done[1][None], done[0][None])
+        parts = [gather_ctx(own, 1) for own in own_parts]
         if groups == 1:
             attended = parts[0]
         else:
-            width = group_heads * HD
             attended = jnp.concatenate(
                 [
                     part[:, side * width : (side + 1) * width]

time: 370 us -> 370 us (level)
  no operation moved by 1% of the time
where the time goes in v1:
time: 370 us
  waiting for transfers between devices  300 us (81%)
  Pallas kernels  20.2 us (5%)
  starting transfers between devices  14.9 us (4%)
  other arithmetic  12.7 us (3%)
  local copies, waits for them, and re-layouts  12.1 us (3%)
  matrix products  8.15 us (2%)
    ppermute x3, waiting for transfers between devices, from_partner(): return lax.ppermute(value, axis, pairs)  274 us
    ppermute x9, waiting for transfers between devices, from_other(): return lax.ppermute(block, 'ctx', [(0, 1), (1, 0)])  25.4 us
    pallas_call x2, Pallas kernels, average_rows(): pl.pallas_call(average_kernel, grid=(rows // tile,), in_specs=specs, out_...  11 us
    ppermute x9, starting transfers between devices, from_other(): return lax.ppermute(block, 'ctx', [(0, 1), (1, 0)])  9.62 us
    pallas_call x2, Pallas kernels, attend(): pl.pallas_call(functools.partial(attend_kernel, step_heads), grid=(heads...  9.22 us
    dot_general x1, matrix products, contract_rows(): lax.dot_general(left_rows, right_rows, (((0,), (0,)), ((), ())), preferre...  8.15 us
  transfers between devices with their start and end apart: 12, of which 9 were waited for; matrix products, arithmetic and copies ran while one was open for 9% of the time, Pallas kernels for 5%

profile of v1, /device:TPU:0, one launch (start us, length us, event | category | flops | bytes accessed | tf_op | source)
XLA Modules:
  0.0 369.6 jit_solution(13282927109436058861)
XLA Ops:
  1.3 368.3 %conditional.1 = (bf16[2048,1024]{1,0:T(8,128)(2,1)}, bf16[2048,1024]{1,0:T(8,128)(2,1)}) conditional(s32[]{:T(128)} %clamp.3, (s32[1]{0:T(128)}, s32[1,2,16]{2,1,0:T(2,128)}, bf16[1,256,2048]{2,1,0:T(8,128)(2,1)}, bf16[1,256,2048]{2,1,0:T(8,128)(2,1)}, bf16[1,256,2048]{2,1,0:T(8,128)(2,1)}, ...), branch_computations={%region_0.1_spmd, %region_1.2_spmd, %region_2.3_spmd, %region_3.4_... | conditional | flops 3264217856 | bytes 155193504 | solution.py:293
  1.8 4.1 %collective-permute-start.36 = (bf16[2048,1024]{1,0:T(8,128)(2,1)}, bf16[2048,1024]{1,0:T(8,128)(2,1)}, u32[]{:S(2)}, u32[]{:S(2)}) collective-permute-start(bf16[2048,1024]{1,0:T(8,128)(2,1)} %bitcast.218), channel_id=1, source_target_pairs={{0,16},{2,18},{4,20},{6,22},{8,24},{10,26},{12,28},{14,30},{16,0},... | collective-permute-start | bytes 12582920 | tf_op jit(solution)/shard_map/cond/branch_3_fun/ppermute | solution.py:26
  5.9 1.9 dynamic-slice_bitcast_fusion.22
  7.8 1.5 collective-permute-start.39
  9.3 1.9 dynamic-slice_bitcast_fusion.21
  11.2 0.5 collective-permute-start.40
  11.7 1.5 collective-permute-start.43
  13.2 0.5 collective-permute-start.37
  13.7 1.3 pad_add_fusion.6.meta
  15.0 2.0 dynamic-slice_bitcast_fusion.23
  17.0 4.2 %slice_bitcast_fusion.4 = bf16[1792,1024]{1,0:T(8,128)(2,1)} fusion(bf16[1,2048,1024]{2,1,0:T(8,128)(2,1)} %get-tuple-element.107), kind=kLoop, calls=%fused_computation.141 | loop fusion | bytes 7340032 | tf_op jit(solution)/shard_map/cond/branch_3_fun/squeeze | solution.py:218
  21.2 1.4 pad_add_fusion.7.meta
  22.6 4.5 %collective-permute-done.37 = s32[2,16]{1,0:T(2,128)S(1)} collective-permute-done((s32[2,16]{1,0:T(2,128)}, s32[2,16]{1,0:T(2,128)S(1)}, u32[]{:S(2)}, u32[]{:S(2)}) %collective-permute-start.37) | collective-permute-done | bytes 160 | tf_op jit(solution)/shard_map/cond/branch_3_fun/ppermute | solution.py:36
  27.1 1.5 collective-permute-start.44
  28.7 0.0 collective-permute-done.39
  28.7 0.4 collective-permute-start.46
  29.1 0.6 fusion.50.scales
  29.6 0.5 collective-permute-start.38
  30.1 1.5 collective-permute-start.42
  31.7 4.9 %collective-permute-done.44 = bf16[256,512]{1,0:T(8,128)(2,1)S(1)} collective-permute-done((bf16[256,512]{1,0:T(8,128)(2,1)}, bf16[256,512]{1,0:T(8,128)(2,1)S(1)}, u32[]{:S(2)}, u32[]{:S(2)}) %collective-permute-start.44) | collective-permute-done | bytes 262176 | tf_op jit(solution)/shard_map/cond/branch_3_fun/ppermute | solution.py:36
  36.5 2.4 bitcast_select_fusion.50
  39.0 0.8 pad_maximum_fusion.19.k_ref
  39.8 0.8 pad_maximum_fusion.20.v_ref
  40.7 1.5 collective-permute-done.38
  42.1 3.4 collective-permute-done.42
  45.5 0.3 bitcast_select_fusion.54
  45.8 0.8 pad_maximum_fusion.18.q_ref
  46.6 4.6 %branch_3_fun.4 = bf16[512,512]{1,0:T(8,128)(2,1)} custom-call(s32[2]{0:T(128)} %pad_add_fusion.6.meta, f32[4,16]{1,0:T(4,128)} %fusion.50.scales, bf16[512,512]{1,0:T(8,128)(2,1)} %pad_maximum_fusion.18.q_ref, bf16[512,512]{1,0:T(8,128)(2,1)} %pad_maximum_fusion.19.k_ref, bf16[512,512]{1,0:T(8,128)(2,1)} %pad_maximum_fusion.20.v_ref), custom_call_target="tpu_custom_call" | custom-call | flops 536870912 | bytes 2097152 | tf_op jit(solution)/shard_map/cond/branch_3_fun/pallas_call | solution.py:110
  51.2 1.5 collective-permute-start.41
  52.7 0.8 pad_maximum_fusion.22.k_ref
  53.6 0.8 pad_maximum_fusion.23.v_ref
  54.4 0.8 pad_maximum_fusion.21.q_ref
  55.2 4.6 %branch_3_fun.5 = bf16[512,512]{1,0:T(8,128)(2,1)} custom-call(s32[2]{0:T(128)} %pad_add_fusion.7.meta, f32[4,16]{1,0:T(4,128)} %fusion.50.scales, bf16[512,512]{1,0:T(8,128)(2,1)} %pad_maximum_fusion.21.q_ref, bf16[512,512]{1,0:T(8,128)(2,1)} %pad_maximum_fusion.22.k_ref, bf16[512,512]{1,0:T(8,128)(2,1)} %pad_maximum_fusion.23.v_ref), custom_call_target="tpu_custom_call" | custom-call | flops 536870912 | bytes 2097152 | tf_op jit(solution)/shard_map/cond/branch_3_fun/pallas_call | solution.py:110
  59.8 0.5 collective-permute-start.45
  60.3 1.3 slice_bitcast_fusion.5
  61.7 0.8 collective-permute-start.35
  62.5 0.6 iota_compare_fusion.3
  63.1 3.1 collective-permute-done.41
  66.2 0.1 broadcast_select_fusion.17
  66.3 8.2 %collective-permute-done.45 = bf16[512,512]{1,0:T(8,128)(2,1)S(1)} collective-permute-done((bf16[512,512]{1,0:T(8,128)(2,1)}, bf16[512,512]{1,0:T(8,128)(2,1)S(1)}, u32[]{:S(2)}, u32[]{:S(2)}) %collective-permute-start.45) | collective-permute-done | bytes 524320 | tf_op jit(solution)/shard_map/cond/branch_3_fun/ppermute | solution.py:36
  74.4 1.1 broadcast_select_fusion.16
  75.6 201.9 %collective-permute-done.36 = bf16[2048,1024]{1,0:T(8,128)(2,1)} collective-permute-done((bf16[2048,1024]{1,0:T(8,128)(2,1)}, bf16[2048,1024]{1,0:T(8,128)(2,1)}, u32[]{:S(2)}, u32[]{:S(2)}) %collective-permute-start.36) | collective-permute-done | bytes 4194336 | tf_op jit(solution)/shard_map/cond/branch_3_fun/ppermute | solution.py:26
  277.4 8.2 %fusion.36.tracker_ref = bf16[2048,1024]{1,0:T(8,128)(2,1)} fusion(bf16[2048,1024]{1,0:T(8,128)(2,1)} %collective-permute-done.36, bf16[1,2048,1024]{2,1,0:T(8,128)(2,1)} %get-tuple-element.115, bf16[512,512]{1,0:T(8,128)(2,1)S(1)} %get-tuple-element.233, bf16[512,512]{1,0:T(8,128)(2,1)S(1)} %get-tuple-element.231, ...), kind=kOutput, calls=%fused_computation.140 | convolution fusion | flops 2173173760 | bytes 19923456 | tf_op jit(solution)/shard_map/cond/branch_3_fun/dot_general | solution.py:30
  285.6 70.5 %collective-permute-done.46.peer_ref = bf16[1792,1024]{1,0:T(8,128)(2,1)} collective-permute-done((bf16[1792,1024]{1,0:T(8,128)(2,1)}, bf16[1792,1024]{1,0:T(8,128)(2,1)}, u32[]{:S(2)}, u32[]{:S(2)}) %collective-permute-start.46) | collective-permute-done | bytes 3670048 | tf_op jit(solution)/shard_map/cond/branch_3_fun/ppermute | solution.py:26
  356.1 8.6 %branch_3_fun.6.rest_0_ = bf16[2048,1024]{1,0:T(8,128)(2,1)} custom-call(bf16[2048,1024]{1,0:T(8,128)(2,1)} %bitcast.207, bf16[1792,1024]{1,0:T(8,128)(2,1)} %collective-permute-done.46.peer_ref, bf16[2048,1024]{1,0:T(8,128)(2,1)} %fusion.36.tracker_ref), custom_call_target="tpu_custom_call" | custom-call | flops 7340032 | bytes 14680064 | tf_op jit(solution)/shard_map/cond/branch_3_fun/pallas_call | solution.py:146
  364.7 1.7 collective-permute-done.35.peer_ref
  366.4 0.8 copy-done.34
  367.2 2.4 branch_3_fun.7
  (26 shorter events, 0.1 us)
Async XLA Ops:
  1.8 275.6 %collective-permute-start.36 = (bf16[2048,1024]{1,0:T(8,128)(2,1)}, bf16[2048,1024]{1,0:T(8,128)(2,1)}, u32[]{:S(2)}, u32[]{:S(2)}) collective-permute-start(bf16[2048,1024]{1,0:T(8,128)(2,1)} %bitcast.218), channel_id=1, source_target_pairs={{0,16},{2,18},{4,20},{6,22},{8,24},{10,26},{12,28},{14,30},{16,0},... | collective-permute-start | bytes 12582920 | tf_op jit(solution)/shard_map/cond/branch_3_fun/ppermute | solution.py:26
  7.8 20.9 %collective-permute-start.39 = (bf16[256,512]{1,0:T(8,128)(2,1)}, bf16[256,512]{1,0:T(8,128)(2,1)S(1)}, u32[]{:S(2)}, u32[]{:S(2)}) collective-permute-start(bf16[256,512]{1,0:T(8,128)(2,1)} %get-tuple-element.240), channel_id=1, source_target_pairs={{0,1},{1,0},{2,3},{3,2},{4,5},{5,4},{6,7},{7,6},{8,9},{9,8},{10,11... | collective-permute-start | bytes 786440 | tf_op jit(solution)/shard_map/cond/branch_3_fun/ppermute | solution.py:36
  11.2 18.5 %collective-permute-start.40 = (bf16[256,512]{1,0:T(8,128)(2,1)}, bf16[256,512]{1,0:T(8,128)(2,1)}, u32[]{:S(2)}, u32[]{:S(2)}) collective-permute-start(bf16[256,512]{1,0:T(8,128)(2,1)} %get-tuple-element.236), channel_id=1, source_target_pairs={{0,1},{1,0},{2,3},{3,2},{4,5},{5,4},{6,7},{7,6},{8,9},{9,8},{10,11... | collective-permute-start | bytes 786440 | tf_op jit(solution)/shard_map/cond/branch_3_fun/ppermute | solution.py:36
  11.7 18.4 %collective-permute-start.43 = (bf16[256,512]{1,0:T(8,128)(2,1)}, bf16[256,512]{1,0:T(8,128)(2,1)}, u32[]{:S(2)}, u32[]{:S(2)}) collective-permute-start(bf16[256,512]{1,0:T(8,128)(2,1)} %get-tuple-element.241), channel_id=1, source_target_pairs={{0,1},{1,0},{2,3},{3,2},{4,5},{5,4},{6,7},{7,6},{8,9},{9,8},{10,11... | collective-permute-start | bytes 786440 | tf_op jit(solution)/shard_map/cond/branch_3_fun/ppermute | solution.py:36
  13.2 13.9 %collective-permute-start.37 = (s32[2,16]{1,0:T(2,128)}, s32[2,16]{1,0:T(2,128)S(1)}, u32[]{:S(2)}, u32[]{:S(2)}) collective-permute-start(s32[2,16]{1,0:T(2,128)} %bitcast.226), channel_id=1, source_target_pairs={{0,1},{1,0},{2,3},{3,2},{4,5},{5,4},{6,7},{7,6},{8,9},{9,8},{10,11... | collective-permute-start | bytes 392 | tf_op jit(solution)/shard_map/cond/branch_3_fun/ppermute | solution.py:36
  15.0 13.7 %copy-start.40 = (s32[1,2,16]{2,1,0:T(2,128)S(1)}, s32[1,2,16]{2,1,0:T(2,128)}, u32[]{:S(2)}) copy-start(s32[1,2,16]{2,1,0:T(2,128)} %get-tuple-element.110) | copy-start | bytes 388 | tf_op jit(solution)/shard_map/cond
  15.0 21.5 %copy-start.5 = (bf16[1,256,2048]{2,1,0:T(8,128)(2,1)S(1)}, bf16[1,256,2048]{2,1,0:T(8,128)(2,1)}, u32[]{:S(2)}) copy-start(bf16[1,256,2048]{2,1,0:T(8,128)(2,1)} %get-tuple-element.112) | copy-start | bytes 3145732 | tf_op jit(solution)/shard_map/cond
  15.0 21.5 %copy-start.8 = (bf16[1,256,2048]{2,1,0:T(8,128)(2,1)S(1)}, bf16[1,256,2048]{2,1,0:T(8,128)(2,1)}, u32[]{:S(2)}) copy-start(bf16[1,256,2048]{2,1,0:T(8,128)(2,1)} %get-tuple-element.113) | copy-start | bytes 3145732 | tf_op jit(solution)/shard_map/cond
  21.2 24.3 %copy-start.12 = (bf16[1,256,2048]{2,1,0:T(8,128)(2,1)S(1)}, bf16[1,256,2048]{2,1,0:T(8,128)(2,1)}, u32[]{:S(2)}) copy-start(bf16[1,256,2048]{2,1,0:T(8,128)(2,1)} %get-tuple-element.111) | copy-start | bytes 3145732 | tf_op jit(solution)/shard_map/cond
  27.1 9.4 %collective-permute-start.44 = (bf16[256,512]{1,0:T(8,128)(2,1)}, bf16[256,512]{1,0:T(8,128)(2,1)S(1)}, u32[]{:S(2)}, u32[]{:S(2)}) collective-permute-start(bf16[256,512]{1,0:T(8,128)(2,1)} %get-tuple-element.237), channel_id=1, source_target_pairs={{0,1},{1,0},{2,3},{3,2},{4,5},{5,4},{6,7},{7,6},{8,9},{9,8},{10,11... | collective-permute-start | bytes 786440 | tf_op jit(solution)/shard_map/cond/branch_3_fun/ppermute | solution.py:36
  28.7 3.0 copy-start.37
  28.7 327.4 %collective-permute-start.46 = (bf16[1792,1024]{1,0:T(8,128)(2,1)}, bf16[1792,1024]{1,0:T(8,128)(2,1)}, u32[]{:S(2)}, u32[]{:S(2)}) collective-permute-start(bf16[1792,1024]{1,0:T(8,128)(2,1)} %slice_bitcast_fusion.4), channel_id=1, source_target_pairs={{0,16},{2,18},{4,20},{6,22},{8,24},{10,26},{12,28},{14,30},{16,0},... | collective-permute-start | bytes 11010056 | tf_op jit(solution)/shard_map/cond/branch_3_fun/ppermute | solution.py:26
  29.6 12.5 %collective-permute-start.38 = (bf16[256,512]{1,0:T(8,128)(2,1)}, bf16[256,512]{1,0:T(8,128)(2,1)S(1)}, u32[]{:S(2)}, u32[]{:S(2)}) collective-permute-start(bf16[256,512]{1,0:T(8,128)(2,1)} %get-tuple-element.244), channel_id=1, source_target_pairs={{0,1},{1,0},{2,3},{3,2},{4,5},{5,4},{6,7},{7,6},{8,9},{9,8},{10,11... | collective-permute-start | bytes 786440 | tf_op jit(solution)/shard_map/cond/branch_3_fun/ppermute | solution.py:36
  30.1 15.4 %collective-permute-start.42 = (bf16[256,512]{1,0:T(8,128)(2,1)}, bf16[256,512]{1,0:T(8,128)(2,1)S(1)}, u32[]{:S(2)}, u32[]{:S(2)}) collective-permute-start(bf16[256,512]{1,0:T(8,128)(2,1)} %get-tuple-element.245), channel_id=1, source_target_pairs={{0,1},{1,0},{2,3},{3,2},{4,5},{5,4},{6,7},{7,6},{8,9},{9,8},{10,11... | collective-permute-start | bytes 786440 | tf_op jit(solution)/shard_map/cond/branch_3_fun/ppermute | solution.py:36
  39.0 13.8 %copy-start.27 = (bf16[256,512]{1,0:T(8,128)(2,1)S(1)}, bf16[256,512]{1,0:T(8,128)(2,1)}, u32[]{:S(2)}) copy-start(bf16[256,512]{1,0:T(8,128)(2,1)} %get-tuple-element.248) | copy-start | bytes 786436 | tf_op jit(solution)/shard_map/cond
  39.0 13.8 %copy-start.28 = (bf16[256,512]{1,0:T(8,128)(2,1)S(1)}, bf16[256,512]{1,0:T(8,128)(2,1)}, u32[]{:S(2)}) copy-start(bf16[256,512]{1,0:T(8,128)(2,1)} %get-tuple-element.249) | copy-start | bytes 786436 | tf_op jit(solution)/shard_map/cond
  39.0 14.6 %copy-start.22 = (bf16[256,512]{1,0:T(8,128)(2,1)S(1)}, bf16[256,512]{1,0:T(8,128)(2,1)}, u32[]{:S(2)}) copy-start(bf16[256,512]{1,0:T(8,128)(2,1)} %get-tuple-element.235) | copy-start | bytes 786436 | tf_op jit(solution)/shard_map/cond
  51.2 15.0 %copy-start.15 = (bf16[512,512]{1,0:T(8,128)(2,1)S(1)}, bf16[512,512]{1,0:T(8,128)(2,1)}, u32[]{:S(2)}) copy-start(bf16[512,512]{1,0:T(8,128)(2,1)} %branch_3_fun.4) | copy-start | bytes 1572868 | tf_op jit(solution)/shard_map/cond
  51.2 15.0 %collective-permute-start.41 = (bf16[512,512]{1,0:T(8,128)(2,1)}, bf16[512,512]{1,0:T(8,128)(2,1)S(1)}, u32[]{:S(2)}, u32[]{:S(2)}) collective-permute-start(bf16[512,512]{1,0:T(8,128)(2,1)} %branch_3_fun.4), channel_id=1, source_target_pairs={{0,1},{1,0},{2,3},{3,2},{4,5},{5,4},{6,7},{7,6},{8,9},{9,8},{10,11... | collective-permute-start | bytes 1572872 | tf_op jit(solution)/shard_map/cond/branch_3_fun/ppermute | solution.py:36
  54.4 223.0 %copy-start.19 = (bf16[1,512,1024]{2,1,0:T(8,128)(2,1)S(1)}, bf16[1,512,1024]{2,1,0:T(8,128)(2,1)}, u32[]{:S(2)}) copy-start(bf16[1,512,1024]{2,1,0:T(8,128)(2,1)} %get-tuple-element.114) | copy-start | bytes 3145732 | tf_op jit(solution)/shard_map/cond
  59.8 217.6 %copy-start.2 = (bf16[1,2048,1024]{2,1,0:T(8,128)(2,1)S(1)}, bf16[1,2048,1024]{2,1,0:T(8,128)(2,1)}, u32[]{:S(2)}) copy-start(bf16[1,2048,1024]{2,1,0:T(8,128)(2,1)} %get-tuple-element.108) | copy-start | bytes 12582916 | tf_op jit(solution)/shard_map/cond
  59.8 14.6 %collective-permute-start.45 = (bf16[512,512]{1,0:T(8,128)(2,1)}, bf16[512,512]{1,0:T(8,128)(2,1)S(1)}, u32[]{:S(2)}, u32[]{:S(2)}) collective-permute-start(bf16[512,512]{1,0:T(8,128)(2,1)} %branch_3_fun.5), channel_id=1, source_target_pairs={{0,1},{1,0},{2,3},{3,2},{4,5},{5,4},{6,7},{7,6},{8,9},{9,8},{10,11... | collective-permute-start | bytes 1572872 | tf_op jit(solution)/shard_map/cond/branch_3_fun/ppermute | solution.py:36
  61.7 304.7 %collective-permute-start.35 = (bf16[256,1024]{1,0:T(8,128)(2,1)S(1)}, bf16[256,1024]{1,0:T(8,128)(2,1)S(1)}, u32[]{:S(2)}, u32[]{:S(2)}) collective-permute-start(bf16[256,1024]{1,0:T(8,128)(2,1)S(1)} %slice_bitcast_fusion.5), channel_id=1, source_target_pairs={{0,16},{2,18},{4,20},{6,22},{8,24},{10,26},{12,28},{14,30},{16,0},... | collective-permute-start | bytes 1572872 | tf_op jit(solution)/shard_map/cond/branch_3_fun/ppermute | solution.py:26
  366.4 0.8 copy-start.34

commit v2 on v1

--- a/solution.py
+++ b/solution.py
@@ -51,12 +51,12 @@
 
 def rows_to_heads(block, group, groups):
     if lax.axis_size("ctx") != 2:
-        return lax.all_to_all(block, "ctx", split_axis=1, concat_axis=0, tiled=True)
+        return (lax.all_to_all(block, "ctx", split_axis=1, concat_axis=0, tiled=True),)
     width = block.shape[1] // (2 * groups)
     mine = lax.axis_index("ctx")
     kept = lax.dynamic_slice_in_dim(block, (mine * groups + group) * width, width, 1)
     sent = lax.dynamic_slice_in_dim(block, ((1 - mine) * groups + group) * width, width, 1)
-    return in_order(kept, from_other(sent), 0)
+    return kept, from_other(sent)
 
 
 def attend_kernel(step_heads, meta, scales, q_ref, k_ref, v_ref, out_ref):
@@ -235,10 +235,15 @@
         mine = lax.axis_index("ctx")
         group_heads = HEADS // (lax.axis_size("ctx") * groups)
         width = group_heads * HD
-        own_parts = [
-            attend(rows, keys, values, scales, length, (mine * groups + group) * group_heads)
-            for group, (keys, values, rows) in enumerate(pieces)
-        ]
+        own_parts = []
+        for group, piece in enumerate(pieces):
+            if own_parts:
+                piece, _ = lax.optimization_barrier((piece, own_parts[-1]))
+            keys, values, rows = (
+                in_order(*halves, 0) if len(halves) == 2 else halves[0] for halves in piece
+            )
+            first_head = (mine * groups + group) * group_heads
+            own_parts.append(attend(rows, keys, values, scales, length, first_head))
         if by_group:
             arrays = (tracker[0], peer_tracker, old_grad[0], params[0], peer_params)
             done = ()

time: 370 us -> 377 us (1.019)
  starting transfers between devices: 14.9 us -> 19.9 us
  waiting for transfers between devices: 300 us -> 304 us
    ppermute x3, waiting for transfers between devices: 274 us -> 290 us  [from_partner(): return lax.ppermute(value, axis, pairs)]
    ppermute x9, waiting for transfers between devices: 25.4 us -> 13.7 us  [from_other(): return lax.ppermute(block, 'ctx', [(0, 1), (1, 0)])]
  transfers between devices with their start and end apart: 12 -> 12, of which waited for: 9 -> 6; matrix products, arithmetic and copies ran while one was open for 9% -> 7% of each run, Pallas kernels for 5% -> 5%
where the time goes in v2:
time: 377 us; the launch traced here: 376 us
  waiting for transfers between devices  304 us (81%)
  Pallas kernels  20.2 us (5%)
  starting transfers between devices  19.9 us (5%)
  other arithmetic  12.3 us (3%)
  local copies, waits for them, and re-layouts  9.66 us (3%)
  matrix products  8.08 us (2%)
    ppermute x3, waiting for transfers between devices, from_partner(): return lax.ppermute(value, axis, pairs)  290 us
    ppermute x9, waiting for transfers between devices, from_other(): return lax.ppermute(block, 'ctx', [(0, 1), (1, 0)])  13.7 us
    ppermute x9, starting transfers between devices, from_other(): return lax.ppermute(block, 'ctx', [(0, 1), (1, 0)])  11.6 us
    pallas_call x2, Pallas kernels, average_rows(): pl.pallas_call(average_kernel, grid=(rows // tile,), in_specs=specs, out_...  11 us
    pallas_call x2, Pallas kernels, attend(): pl.pallas_call(functools.partial(attend_kernel, step_heads), grid=(heads...  9.19 us
    ppermute x3, starting transfers between devices, from_partner(): return lax.ppermute(value, axis, pairs)  8.26 us
    dot_general x1, matrix products, contract_rows(): lax.dot_general(left_rows, right_rows, (((0,), (0,)), ((), ())), preferre...  8.08 us
  transfers between devices with their start and end apart: 12, of which 6 were waited for; matrix products, arithmetic and copies ran while one was open for 7% of the time, Pallas kernels for 5%

profile of v2, /device:TPU:0, one launch (start us, length us, event | category | flops | bytes accessed | tf_op | source)
XLA Modules:
  0.0 376.2 jit_solution(10149215670211376814)
XLA Ops:
  1.3 374.9 %conditional.1 = (bf16[2048,1024]{1,0:T(8,128)(2,1)}, bf16[2048,1024]{1,0:T(8,128)(2,1)}) conditional(s32[]{:T(128)} %clamp.3, (s32[1]{0:T(128)}, s32[1,2,16]{2,1,0:T(2,128)}, bf16[1,256,2048]{2,1,0:T(8,128)(2,1)}, bf16[1,256,2048]{2,1,0:T(8,128)(2,1)}, bf16[1,256,2048]{2,1,0:T(8,128)(2,1)}, ...), branch_computations={%region_0.1_spmd, %region_1.2_spmd, %region_2.3_spmd, %region_3.4_... | conditional | flops 3264217856 | bytes 139988976 | solution.py:298
  1.8 0.0 copy-start.20
  1.8 1.2 dynamic-slice_bitcast_fusion.34
  3.0 3.1 collective-permute-start.39
  6.1 1.2 dynamic-slice_bitcast_fusion.33
  7.2 0.1 collective-permute-start.40
  7.3 1.2 dynamic-slice_bitcast_fusion.35
  8.5 2.1 collective-permute-start.38
  10.6 0.1 collective-permute-start.37
  10.6 3.0 collective-permute-start.36
  13.7 1.2 pad_add_fusion.6.meta
  14.9 1.3 pad_add_fusion.7.meta
  16.1 4.2 %slice_bitcast_fusion.4 = bf16[1792,1024]{1,0:T(8,128)(2,1)} fusion(bf16[1,2048,1024]{2,1,0:T(8,128)(2,1)} %get-tuple-element.125), kind=kLoop, calls=%fused_computation.150 | loop fusion | bytes 7340032 | tf_op jit(solution)/shard_map/cond/branch_3_fun/squeeze | solution.py:218
  20.4 3.3 collective-permute-done.37
  23.7 1.7 collective-permute-start.42
  25.4 0.6 fusion.50.scales
  26.0 0.0 collective-permute-done.38
  26.0 0.3 collective-permute-start.43
  26.3 1.0 bitcast_select_fusion.30
  27.3 0.0 collective-permute-done.39
  27.3 1.8 collective-permute-start.44
  29.1 2.6 collective-permute-start.46
  31.7 1.3 bitcast_select_fusion.26
  33.0 0.9 pad_maximum_fusion.19.k_ref
  33.9 0.8 pad_maximum_fusion.20.v_ref
  34.7 0.8 pad_maximum_fusion.18.q_ref
  35.5 4.6 %branch_3_fun.4 = bf16[512,512]{1,0:T(8,128)(2,1)} custom-call(s32[2]{0:T(128)} %pad_add_fusion.6.meta, f32[4,16]{1,0:T(4,128)} %fusion.50.scales, bf16[512,512]{1,0:T(8,128)(2,1)} %pad_maximum_fusion.18.q_ref, bf16[512,512]{1,0:T(8,128)(2,1)} %pad_maximum_fusion.19.k_ref, bf16[512,512]{1,0:T(8,128)(2,1)} %pad_maximum_fusion.20.v_ref), custom_call_target="tpu_custom_call" | custom-call | flops 536870912 | bytes 2097152 | tf_op jit(solution)/shard_map/cond/branch_3_fun/pallas_call | solution.py:110
  40.1 0.5 collective-permute-start.41
  40.6 3.2 collective-permute-done.44
  43.9 0.8 pad_maximum_fusion.23.v_ref
  44.7 0.8 pad_maximum_fusion.22.k_ref
  45.6 0.0 copy-start.9
  45.6 0.8 pad_maximum_fusion.21.q_ref
  46.4 4.6 %branch_3_fun.5 = bf16[512,512]{1,0:T(8,128)(2,1)} custom-call(s32[2]{0:T(128)} %pad_add_fusion.7.meta, f32[4,16]{1,0:T(4,128)} %fusion.50.scales, bf16[512,512]{1,0:T(8,128)(2,1)} %pad_maximum_fusion.21.q_ref, bf16[512,512]{1,0:T(8,128)(2,1)} %pad_maximum_fusion.22.k_ref, bf16[512,512]{1,0:T(8,128)(2,1)} %pad_maximum_fusion.23.v_ref), custom_call_target="tpu_custom_call" | custom-call | flops 536870912 | bytes 2097152 | tf_op jit(solution)/shard_map/cond/branch_3_fun/pallas_call | solution.py:110
  51.1 2.0 collective-permute-start.45
  53.1 1.1 slice_bitcast_fusion.5
  54.1 2.7 collective-permute-start.35
  56.8 0.6 iota_compare_fusion.3
  57.5 0.1 broadcast_select_fusion.35
  57.6 7.2 %collective-permute-done.45 = bf16[512,512]{1,0:T(8,128)(2,1)S(1)} collective-permute-done((bf16[512,512]{1,0:T(8,128)(2,1)}, bf16[512,512]{1,0:T(8,128)(2,1)S(1)}, u32[]{:S(2)}, u32[]{:S(2)}) %collective-permute-start.45) | collective-permute-done | bytes 524320 | tf_op jit(solution)/shard_map/cond/branch_3_fun/ppermute | solution.py:36
  64.8 1.1 broadcast_select_fusion.34
  65.9 218.4 %collective-permute-done.36 = bf16[2048,1024]{1,0:T(8,128)(2,1)} collective-permute-done((bf16[2048,1024]{1,0:T(8,128)(2,1)}, bf16[2048,1024]{1,0:T(8,128)(2,1)}, u32[]{:S(2)}, u32[]{:S(2)}) %collective-permute-start.36) | collective-permute-done | bytes 4194336 | tf_op jit(solution)/shard_map/cond/branch_3_fun/ppermute | solution.py:26
  284.3 8.1 %fusion.36.tracker_ref = bf16[2048,1024]{1,0:T(8,128)(2,1)} fusion(bf16[2048,1024]{1,0:T(8,128)(2,1)} %collective-permute-done.36, bf16[1,2048,1024]{2,1,0:T(8,128)(2,1)S(1)} %copy-done.2, bf16[512,512]{1,0:T(8,128)(2,1)S(1)} %get-tuple-element.236, bf16[512,512]{1,0:T(8,128)(2,1)S(1)} %get-tuple-element.234, bf16[512,512]{1,0:T(8,128)(2,1)S(1)} %get-tuple-element.235, ...), kind=kOutput, calls=%fused_computation.149 | convolution fusion | flops 2173173760 | bytes 19923456 | tf_op jit(solution)/shard_map/cond/branch_3_fun/dot_general | solution.py:30
  292.4 70.6 %collective-permute-done.46.peer_ref = bf16[1792,1024]{1,0:T(8,128)(2,1)} collective-permute-done((bf16[1792,1024]{1,0:T(8,128)(2,1)}, bf16[1792,1024]{1,0:T(8,128)(2,1)}, u32[]{:S(2)}, u32[]{:S(2)}) %collective-permute-start.46) | collective-permute-done | bytes 3670048 | tf_op jit(solution)/shard_map/cond/branch_3_fun/ppermute | solution.py:26
  363.0 8.6 %branch_3_fun.6.rest_0_ = bf16[2048,1024]{1,0:T(8,128)(2,1)} custom-call(bf16[2048,1024]{1,0:T(8,128)(2,1)} %bitcast.195, bf16[1792,1024]{1,0:T(8,128)(2,1)} %collective-permute-done.46.peer_ref, bf16[2048,1024]{1,0:T(8,128)(2,1)} %fusion.36.tracker_ref), custom_call_target="tpu_custom_call" | custom-call | flops 7340032 | bytes 14680064 | tf_op jit(solution)/shard_map/cond/branch_3_fun/pallas_call | solution.py:146
  371.6 1.4 collective-permute-done.35.peer_ref
  373.0 0.8 copy-done.14
  373.8 2.4 branch_3_fun.7
  (15 shorter events, 0.1 us)
Async XLA Ops:
  1.8 8.7 %copy-start.20 = (s32[1,2,16]{2,1,0:T(2,128)S(1)}, s32[1,2,16]{2,1,0:T(2,128)}, u32[]{:S(2)}) copy-start(s32[1,2,16]{2,1,0:T(2,128)} %get-tuple-element.128) | copy-start | bytes 388 | tf_op jit(solution)/shard_map/cond
  3.0 24.3 %collective-permute-start.39 = (bf16[256,512]{1,0:T(8,128)(2,1)S(1)}, bf16[256,512]{1,0:T(8,128)(2,1)S(1)}, u32[]{:S(2)}, u32[]{:S(2)}) collective-permute-start(bf16[256,512]{1,0:T(8,128)(2,1)S(1)} %get-tuple-element.240), channel_id=1, source_target_pairs={{0,1},{1,0},{2,3},{3,2},{4,5},{5,4},{6,7},{7,6},{8,9},{9,8},{10,11... | collective-permute-start | bytes 786440 | tf_op jit(solution)/shard_map/cond/branch_3_fun/ppermute | solution.py:36
  7.2 21.9 %collective-permute-start.40 = (bf16[256,512]{1,0:T(8,128)(2,1)S(1)}, bf16[256,512]{1,0:T(8,128)(2,1)}, u32[]{:S(2)}, u32[]{:S(2)}) collective-permute-start(bf16[256,512]{1,0:T(8,128)(2,1)S(1)} %get-tuple-element.237), channel_id=1, source_target_pairs={{0,1},{1,0},{2,3},{3,2},{4,5},{5,4},{6,7},{7,6},{8,9},{9,8},{10,11... | collective-permute-start | bytes 786440 | tf_op jit(solution)/shard_map/cond/branch_3_fun/ppermute | solution.py:36
  8.5 17.5 %collective-permute-start.38 = (bf16[256,512]{1,0:T(8,128)(2,1)S(1)}, bf16[256,512]{1,0:T(8,128)(2,1)S(1)}, u32[]{:S(2)}, u32[]{:S(2)}) collective-permute-start(bf16[256,512]{1,0:T(8,128)(2,1)S(1)} %get-tuple-element.243), channel_id=1, source_target_pairs={{0,1},{1,0},{2,3},{3,2},{4,5},{5,4},{6,7},{7,6},{8,9},{9,8},{10,11... | collective-permute-start | bytes 786440 | tf_op jit(solution)/shard_map/cond/branch_3_fun/ppermute | solution.py:36
  10.6 13.1 %collective-permute-start.37 = (s32[2,16]{1,0:T(2,128)S(1)}, s32[2,16]{1,0:T(2,128)S(1)}, u32[]{:S(2)}, u32[]{:S(2)}) collective-permute-start(s32[2,16]{1,0:T(2,128)S(1)} %bitcast.206), channel_id=1, source_target_pairs={{0,1},{1,0},{2,3},{3,2},{4,5},{5,4},{6,7},{7,6},{8,9},{9,8},{10,11... | collective-permute-start | bytes 392 | tf_op jit(solution)/shard_map/cond/branch_3_fun/ppermute | solution.py:36
  10.6 273.7 %collective-permute-start.36 = (bf16[2048,1024]{1,0:T(8,128)(2,1)}, bf16[2048,1024]{1,0:T(8,128)(2,1)}, u32[]{:S(2)}, u32[]{:S(2)}) collective-permute-start(bf16[2048,1024]{1,0:T(8,128)(2,1)} %bitcast.70), channel_id=1, source_target_pairs={{0,16},{2,18},{4,20},{6,22},{8,24},{10,26},{12,28},{14,30},{16,0},... | collective-permute-start | bytes 12582920 | tf_op jit(solution)/shard_map/cond/branch_3_fun/ppermute | solution.py:26
  23.7 16.5 %collective-permute-start.42 = (bf16[256,512]{1,0:T(8,128)(2,1)S(1)}, bf16[256,512]{1,0:T(8,128)(2,1)S(1)}, u32[]{:S(2)}, u32[]{:S(2)}) collective-permute-start(bf16[256,512]{1,0:T(8,128)(2,1)S(1)} %get-tuple-element.241), channel_id=1, source_target_pairs={{0,1},{1,0},{2,3},{3,2},{4,5},{5,4},{6,7},{7,6},{8,9},{9,8},{10,11... | collective-permute-start | bytes 786440 | tf_op jit(solution)/shard_map/cond/branch_3_fun/ppermute | solution.py:36
  26.0 14.7 %collective-permute-start.43 = (bf16[256,512]{1,0:T(8,128)(2,1)S(1)}, bf16[256,512]{1,0:T(8,128)(2,1)S(1)}, u32[]{:S(2)}, u32[]{:S(2)}) collective-permute-start(bf16[256,512]{1,0:T(8,128)(2,1)S(1)} %get-tuple-element.238), channel_id=1, source_target_pairs={{0,1},{1,0},{2,3},{3,2},{4,5},{5,4},{6,7},{7,6},{8,9},{9,8},{10,11... | collective-permute-start | bytes 786440 | tf_op jit(solution)/shard_map/cond/branch_3_fun/ppermute | solution.py:36
  27.3 16.5 %collective-permute-start.44 = (bf16[256,512]{1,0:T(8,128)(2,1)S(1)}, bf16[256,512]{1,0:T(8,128)(2,1)S(1)}, u32[]{:S(2)}, u32[]{:S(2)}) collective-permute-start(bf16[256,512]{1,0:T(8,128)(2,1)S(1)} %get-tuple-element.244), channel_id=1, source_target_pairs={{0,1},{1,0},{2,3},{3,2},{4,5},{5,4},{6,7},{7,6},{8,9},{9,8},{10,11... | collective-permute-start | bytes 786440 | tf_op jit(solution)/shard_map/cond/branch_3_fun/ppermute | solution.py:36
  29.1 333.9 %collective-permute-start.46 = (bf16[1792,1024]{1,0:T(8,128)(2,1)}, bf16[1792,1024]{1,0:T(8,128)(2,1)}, u32[]{:S(2)}, u32[]{:S(2)}) collective-permute-start(bf16[1792,1024]{1,0:T(8,128)(2,1)} %slice_bitcast_fusion.4), channel_id=1, source_target_pairs={{0,16},{2,18},{4,20},{6,22},{8,24},{10,26},{12,28},{14,30},{16,0},... | collective-permute-start | bytes 11010056 | tf_op jit(solution)/shard_map/cond/branch_3_fun/ppermute | solution.py:26
  40.1 17.3 %collective-permute-start.41 = (bf16[512,512]{1,0:T(8,128)(2,1)}, bf16[512,512]{1,0:T(8,128)(2,1)S(1)}, u32[]{:S(2)}, u32[]{:S(2)}) collective-permute-start(bf16[512,512]{1,0:T(8,128)(2,1)} %branch_3_fun.4), channel_id=1, source_target_pairs={{0,1},{1,0},{2,3},{3,2},{4,5},{5,4},{6,7},{7,6},{8,9},{9,8},{10,11... | collective-permute-start | bytes 1572872 | tf_op jit(solution)/shard_map/cond/branch_3_fun/ppermute | solution.py:36
  43.9 13.6 %copy-start.5 = (bf16[512,512]{1,0:T(8,128)(2,1)S(1)}, bf16[512,512]{1,0:T(8,128)(2,1)}, u32[]{:S(2)}) copy-start(bf16[512,512]{1,0:T(8,128)(2,1)} %branch_3_fun.4) | copy-start | bytes 1572868 | tf_op jit(solution)/shard_map/cond
  45.6 238.7 %copy-start.9 = (bf16[1,512,1024]{2,1,0:T(8,128)(2,1)S(1)}, bf16[1,512,1024]{2,1,0:T(8,128)(2,1)}, u32[]{:S(2)}) copy-start(bf16[1,512,1024]{2,1,0:T(8,128)(2,1)} %get-tuple-element.138) | copy-start | bytes 3145732 | tf_op jit(solution)/shard_map/cond
  51.0 233.3 %copy-start.2 = (bf16[1,2048,1024]{2,1,0:T(8,128)(2,1)S(1)}, bf16[1,2048,1024]{2,1,0:T(8,128)(2,1)}, u32[]{:S(2)}) copy-start(bf16[1,2048,1024]{2,1,0:T(8,128)(2,1)} %get-tuple-element.139) | copy-start | bytes 12582916 | tf_op jit(solution)/shard_map/cond
  51.1 13.8 %collective-permute-start.45 = (bf16[512,512]{1,0:T(8,128)(2,1)}, bf16[512,512]{1,0:T(8,128)(2,1)S(1)}, u32[]{:S(2)}, u32[]{:S(2)}) collective-permute-start(bf16[512,512]{1,0:T(8,128)(2,1)} %branch_3_fun.5), channel_id=1, source_target_pairs={{0,1},{1,0},{2,3},{3,2},{4,5},{5,4},{6,7},{7,6},{8,9},{9,8},{10,11... | collective-permute-start | bytes 1572872 | tf_op jit(solution)/shard_map/cond/branch_3_fun/ppermute | solution.py:36
  54.1 318.8 %collective-permute-start.35 = (bf16[256,1024]{1,0:T(8,128)(2,1)S(1)}, bf16[256,1024]{1,0:T(8,128)(2,1)S(1)}, u32[]{:S(2)}, u32[]{:S(2)}) collective-permute-start(bf16[256,1024]{1,0:T(8,128)(2,1)S(1)} %slice_bitcast_fusion.5), channel_id=1, source_target_pairs={{0,16},{2,18},{4,20},{6,22},{8,24},{10,26},{12,28},{14,30},{16,0},... | collective-permute-start | bytes 1572872 | tf_op jit(solution)/shard_map/cond/branch_3_fun/ppermute | solution.py:26
  373.0 0.8 copy-start.14
